TPU v7x, 32 devices: a whole 2x2x4 slice. The times are simulated.
32 devices in a mesh: rows: 8 (over y, x, core), tp: 4 (over z).
Axes of the slice: x: 2, y: 2, z: 4, core: 2. Of those that a mesh axis runs over, the one named last changes fastest.
Arguments:
- hidden: bfloat16 [2048, 8, 1024], P('tp', 'rows'), may hold values from -6 to 6
- cotangent: bfloat16 [2048, 8, 1024], P('tp', 'rows'), may hold values from -6 to 6
- pair_lengths: int32 [8, 12], P('rows'), may hold values from 1 to 512, 2048 in all within a row
- w_qkv: bfloat16 [3, 1024, 1024], P(None, 'rows', 'tp'), may hold values from -0.1875 to 0.1875
- qkv_bias: bfloat16 [3, 1024], P(None, 'tp'), may hold values from -3 to 3
- w_out: bfloat16 [1024, 1024], P('tp', 'rows'), may hold values from -1.5 to 1.5
- w_up: bfloat16 [1024, 4096], P('rows', 'tp'), may hold values from -0.1875 to 0.1875
- up_bias: bfloat16 [4096], P('tp'), may hold values from -3 to 3
- w_down: bfloat16 [4096, 1024], P('tp', 'rows'), may hold values from -0.09375 to 0.09375
- resid_bias: bfloat16 [2, 1024], replicated, may hold values from -3 to 3
- norm_gain: bfloat16 [2, 1024], replicated, may hold values from 0.5 to 1.5
- norm_bias: bfloat16 [2, 1024], replicated, may hold values from -2 to 2
- prefix_keys: bfloat16 [64, 1024], P(None, 'tp'), may hold values from -6 to 6
- prefix_values: bfloat16 [64, 1024], P(None, 'tp'), may hold values from -6 to 6
Outputs:
- result: bfloat16 [2048, 8, 1024], P('tp', 'rows')
- grad_input: float32 [2048, 8, 1024], P('tp', 'rows')
- key_total: float32 [64, 1024], P(None, 'tp')
- value_total: float32 [64, 1024], P(None, 'tp')
Inputs may be any that keep to these rules, and one draw needn't show every extreme that they name: Each row of pair_lengths holds 11 pair lengths followed by the length of the trailing pad; a row's entries sum to 2048 and its largest is exactly 512.
All inputs are finite; a program needn't handle non-finite values.
Results may differ from a plain program's by a relative error of at most 0.015.
Values may be sent and summed in bfloat16 or wider, within the bound.
No kernel may reach another device: no remote copies, remote signals or barrier semaphores. Data moves between devices by JAX's collectives and lax.ppermute only.
A program may use at most 128 MiB of HBM per device.

v0:
```python
from functools import partial
import jax
import jax.numpy as jnp
from jax import lax
from jax.sharding import PartitionSpec as P

HEAD_DIM = 64
PREFIX = 64
SEQ = 2048
QBLOCK = 512
EPS = 1e-05
NEG = -1e30


def layer_norm(values, gain, shift):
    mean = jnp.mean(values, axis=-1, keepdims=True)
    centred = values - mean
    variance = jnp.mean(centred * centred, axis=-1, keepdims=True)
    return centred * lax.rsqrt(variance + EPS) * gain + shift


def norm_back(values, gain, shift, grad):
    unused, pull = jax.vjp(lambda inner: layer_norm(inner, gain, shift), values)
    return pull(grad)[0]


def segment_ids(pair_lengths):
    ends = jnp.cumsum(pair_lengths, axis=-1)
    place = jnp.arange(SEQ, dtype=jnp.int32)
    return jnp.sum((place[None, :, None] >= ends[:, None, :]).astype(jnp.int32), axis=-1)


def block_scores(query_block, keys_all, seg_block, key_seg, pad_id):
    scale = HEAD_DIM ** (-0.5)
    scores = (
        jnp.einsum("qhd,khd->hqk", query_block, keys_all, preferred_element_type=jnp.float32)
        * scale
    )
    is_prefix = jnp.arange(key_seg.shape[0], dtype=jnp.int32) < PREFIX
    allowed = is_prefix[None, :] | (key_seg[None, :] == seg_block[:, None]) & (
        seg_block[:, None] != pad_id
    )
    return jnp.where(allowed[None], scores, NEG)


def row_parts(packed_row, seg_row, key_prefix, value_prefix):
    keys_all = jnp.concatenate([key_prefix, packed_row[:, 1]], axis=0)
    values_all = jnp.concatenate([value_prefix, packed_row[:, 2]], axis=0)
    key_seg = jnp.concatenate([jnp.full((PREFIX,), -1, jnp.int32), seg_row])
    return (packed_row[:, 0], keys_all, values_all, key_seg)


def attend_row(packed_row, seg_row, key_prefix, value_prefix, pad_id):
    queries, keys_all, values_all, key_seg = row_parts(
        packed_row, seg_row, key_prefix, value_prefix
    )
    blocks = SEQ // QBLOCK
    heads_here = queries.shape[1]

    def one(args):
        query_block, seg_block = args
        scores = block_scores(query_block, keys_all, seg_block, key_seg, pad_id)
        peak = jnp.max(scores, axis=-1, keepdims=True)
        expo = jnp.exp(scores - peak)
        total = jnp.sum(expo, axis=-1, keepdims=True)
        probs = (expo / total).astype(jnp.bfloat16)
        mixed = jnp.einsum("hqk,khd->qhd", probs, values_all, preferred_element_type=jnp.float32)
        return (mixed.astype(jnp.bfloat16), (peak + jnp.log(total))[..., 0])

    mixed, logsum = lax.map(
        one,
        (queries.reshape(blocks, QBLOCK, heads_here, HEAD_DIM), seg_row.reshape(blocks, QBLOCK)),
    )
    return (mixed.reshape(SEQ, heads_here * HEAD_DIM), logsum)


def attend_back(packed_row, seg_row, grad_row, logsum, key_prefix, value_prefix, pad_id):
    queries, keys_all, values_all, key_seg = row_parts(
        packed_row, seg_row, key_prefix, value_prefix
    )
    blocks = SEQ // QBLOCK
    heads_here = queries.shape[1]
    scale = HEAD_DIM ** (-0.5)

    def one(carry, args):
        key_acc, value_acc = carry
        query_block, seg_block, grad_block, sums = args
        scores = block_scores(query_block, keys_all, seg_block, key_seg, pad_id)
        probs = jnp.exp(scores - sums[:, :, None])
        dprobs = jnp.einsum(
            "qhd,khd->hqk", grad_block, values_all, preferred_element_type=jnp.float32
        )
        inner = jnp.sum(probs * dprobs, axis=-1, keepdims=True)
        dscores = (probs * (dprobs - inner)).astype(jnp.bfloat16)
        query_grad = (
            jnp.einsum("hqk,khd->qhd", dscores, keys_all, preferred_element_type=jnp.float32)
            * scale
        )
        key_acc = (
            key_acc
            + jnp.einsum("hqk,qhd->khd", dscores, query_block, preferred_element_type=jnp.float32)
            * scale
        )
        value_acc = value_acc + jnp.einsum(
            "hqk,qhd->khd",
            probs.astype(jnp.bfloat16),
            grad_block,
            preferred_element_type=jnp.float32,
        )
        return ((key_acc, value_acc), query_grad.astype(jnp.bfloat16))

    start_acc = (jnp.zeros(keys_all.shape, jnp.float32), jnp.zeros(values_all.shape, jnp.float32))
    inputs = (
        queries.reshape(blocks, QBLOCK, heads_here, HEAD_DIM),
        seg_row.reshape(blocks, QBLOCK),
        grad_row.reshape(blocks, QBLOCK, heads_here, HEAD_DIM),
        logsum,
    )
    (key_acc, value_acc), query_grads = lax.scan(one, start_acc, inputs)
    grad_packed = jnp.stack(
        [
            query_grads.reshape(SEQ, heads_here, HEAD_DIM),
            key_acc[PREFIX:].astype(jnp.bfloat16),
            value_acc[PREFIX:].astype(jnp.bfloat16),
        ],
        axis=1,
    )
    return (grad_packed, key_acc[:PREFIX], value_acc[:PREFIX])


def collect(w_qkv, w_out, w_up, w_down):
    return (
        lax.all_gather(w_qkv, "rows", axis=1, tiled=True),
        lax.all_gather(w_out, "rows", axis=1, tiled=True),
        lax.all_gather(w_up, "rows", axis=0, tiled=True),
        lax.all_gather(w_down, "rows", axis=1, tiled=True),
    )


def project_inputs(hidden, qkv_full, qkv_shift):
    piece = lax.all_gather(hidden, "tp", axis=0, tiled=True)
    mixed = (
        jnp.einsum("nrd,jde->nrje", piece, qkv_full, preferred_element_type=jnp.float32) + qkv_shift
    )
    return mixed.astype(jnp.bfloat16).reshape(piece.shape[0], piece.shape[1], -1)


def expand(normed_low, up_full, up_shift):
    return (
        jnp.einsum(
            "nrd,df->nrf",
            lax.all_gather(normed_low, "tp", axis=0, tiled=True),
            up_full,
            preferred_element_type=jnp.float32,
        )
        + up_shift
    )


def mix_heads(mixed, out_full):
    return lax.psum_scatter(
        jnp.einsum("nrk,kd->nrd", mixed, out_full, preferred_element_type=jnp.float32),
        "tp",
        scatter_dimension=0,
        tiled=True,
    )


def reduce_down(active, down_full):
    return lax.psum_scatter(
        jnp.einsum("nrf,fd->nrd", active, down_full, preferred_element_type=jnp.float32),
        "tp",
        scatter_dimension=0,
        tiled=True,
    )


def output_back(grad_low, down_full, expanded):
    grad_active = jnp.einsum(
        "nrd,fd->nrf",
        lax.all_gather(grad_low, "tp", axis=0, tiled=True),
        down_full,
        preferred_element_type=jnp.float32,
    )
    unused, pull = jax.vjp(partial(jax.nn.gelu, approximate=False), expanded)
    return pull(grad_active)[0].astype(jnp.bfloat16)


def up_back(grad_hidden, up_full):
    return lax.psum_scatter(
        jnp.einsum("nrf,df->nrd", grad_hidden, up_full, preferred_element_type=jnp.float32),
        "tp",
        scatter_dimension=0,
        tiled=True,
    )


def mixing_back(grad_low, out_full):
    return jnp.einsum(
        "nrd,kd->nrk",
        lax.all_gather(grad_low, "tp", axis=0, tiled=True),
        out_full,
        preferred_element_type=jnp.float32,
    ).astype(jnp.bfloat16)


def input_back(grad_packed, qkv_full, local_rows):
    piece = grad_packed
    piece = piece.reshape(lax.axis_size("tp") * local_rows, piece.shape[1], 3, -1)
    return lax.psum_scatter(
        jnp.einsum("nrje,jde->nrd", piece, qkv_full, preferred_element_type=jnp.float32).astype(
            jnp.bfloat16
        ),
        "tp",
        scatter_dimension=0,
        tiled=True,
    ).astype(jnp.float32)


def body(
    hidden,
    cotangent,
    pair_lengths,
    w_qkv,
    qkv_bias,
    w_out,
    w_up,
    up_bias,
    w_down,
    resid_bias,
    norm_gain,
    norm_bias,
    prefix_keys,
    prefix_values,
):
    local_rows = hidden.shape[0]
    row_count = hidden.shape[1]
    width = w_qkv.shape[2]
    heads_here = width // HEAD_DIM
    pad_id = pair_lengths.shape[1] - 1
    seg = segment_ids(pair_lengths)
    shifts = resid_bias.astype(jnp.float32)
    gains = norm_gain.astype(jnp.float32)
    offsets = norm_bias.astype(jnp.float32)
    qkv_shift = qkv_bias.astype(jnp.float32)
    up_shift = up_bias.astype(jnp.float32)
    key_prefix = prefix_keys.reshape(PREFIX, heads_here, HEAD_DIM)
    value_prefix = prefix_values.reshape(PREFIX, heads_here, HEAD_DIM)

    def heads_of(packed):
        return jnp.moveaxis(packed.reshape(SEQ, row_count, 3, heads_here, HEAD_DIM), 1, 0)

    qkv_full, out_full, up_full, down_full = collect(w_qkv, w_out, w_up, w_down)
    packed = project_inputs(hidden, qkv_full, qkv_shift)
    mixed, logsum = lax.map(
        lambda args: attend_row(args[0], args[1], key_prefix, value_prefix, pad_id),
        (heads_of(packed), seg),
    )
    attended = mix_heads(jnp.moveaxis(mixed, 0, 1), out_full)
    first = hidden.astype(jnp.float32) + attended + shifts[0]
    normed = layer_norm(first, gains[0], offsets[0])
    normed_low = normed.astype(jnp.bfloat16)
    expanded = expand(normed_low, up_full, up_shift)
    active = jax.nn.gelu(expanded, approximate=False).astype(jnp.bfloat16)
    second = normed + reduce_down(active, down_full) + shifts[1]
    result = layer_norm(second, gains[1], offsets[1])
    qkv_full, out_full, up_full, down_full = collect(w_qkv, w_out, w_up, w_down)
    packed = project_inputs(hidden, qkv_full, qkv_shift)
    expanded = expand(normed_low, up_full, up_shift)
    grad_second = norm_back(second, gains[1], offsets[1], cotangent.astype(jnp.float32))
    grad_hidden = output_back(grad_second.astype(jnp.bfloat16), down_full, expanded)
    grad_normed = up_back(grad_hidden, up_full) + grad_second
    grad_first = norm_back(first, gains[0], offsets[0], grad_normed)
    grad_mixed = mixing_back(grad_first.astype(jnp.bfloat16), out_full)
    grad_rows = jnp.moveaxis(grad_mixed, 1, 0).reshape(row_count, SEQ, heads_here, HEAD_DIM)
    grad_packed, key_grads, value_grads = lax.map(
        lambda args: attend_back(
            args[0], args[1], args[2], args[3], key_prefix, value_prefix, pad_id
        ),
        (heads_of(packed), seg, grad_rows, logsum),
    )
    grad_packed = jnp.moveaxis(grad_packed, 0, 1).reshape(SEQ, row_count, 3 * width)
    grad_input = input_back(grad_packed, qkv_full, local_rows) + grad_first
    key_local = jnp.sum(key_grads, axis=0).reshape(PREFIX, width)
    value_local = jnp.sum(value_grads, axis=0).reshape(PREFIX, width)
    key_total, value_total = (
        lax.psum(key_local.astype(jnp.bfloat16), "rows").astype(jnp.float32),
        lax.psum(value_local.astype(jnp.bfloat16), "rows").astype(jnp.float32),
    )
    return (result.astype(jnp.bfloat16), grad_input, key_total, value_total)


def solution(mesh):
    placed = (
        P("tp", "rows", None),
        P("tp", "rows", None),
        P("rows", None),
        P(None, "rows", "tp"),
        P(None, "tp"),
        P("tp", "rows"),
        P("rows", "tp"),
        P("tp"),
        P("tp", "rows"),
        P(),
        P(),
        P(),
        P(None, "tp"),
        P(None, "tp"),
    )
    return jax.shard_map(
        body,
        mesh=mesh,
        in_specs=placed,
        out_specs=(P("tp", "rows", None), P("tp", "rows", None), P(None, "tp"), P(None, "tp")),
        check_vma=False,
    )
```

profile of v0, /device:TPU:0, one launch (start us, length us, event | category | flops | bytes accessed | tf_op | source)
XLA Modules:
  0.0 1455.1 jit_solution(514246632856984945)
XLA Ops:
  13.4 14.6 %all_gather.32 = bf16[256,1024]{1,0:T(8,128)(2,1)} all-gather(bf16[256,128]{1,0:T(8,128)(2,1)} %param.23), channel_id=1, replica_groups=mesh['rows'=8,'tp'=4] {'rows'}, dimensions={1}, use_global_device_ids=true | all-gather | bytes 589824 | tf_op jit(solution)/shard_map/all_gather | solution.py:134
  40.3 82.3 %all-gather.8.cloned.1.call-done = bf16[2048,1,1024]{2,0,1:T(8,128)(2,1)} async-done(((bf16[512,1,1024]{2,0,1:T(8,128)(2,1)}), bf16[2048,1,1024]{2,0,1:T(8,128)(2,1)}) %all-gather.8.cloned.1.call-update) | async-done | bytes 4194320 | tf_op jit(solution)/shard_map/all_gather | solution.py:141
  135.6 120.9 %while.47 = (s32[]{:T(128)}, bf16[4,512,4,64]{1,3,2,0:T(8,128)(2,1)}, f32[4,4,512]{2,1,0:T(4,128)S(1)}, s32[2112]{0:T(1024)S(1)}, s32[4,512]{1,0:T(4,128)S(1)}, ...) while((s32[]{:T(128)}, ...), condition=%wide.region_5.6_spmd, body=%wide.region_2.5_spmd.sunk | while | flops 1162576384 | bytes 59005412 | solution.py:70
  264.2 142.6 %reduce-scatter.5.cloned.1.call-done = f32[512,1,1024]{2,0,1:T(8,128)} async-done(((f32[2048,1,1024]{2,0,1:T(8,128)}), f32[512,1,1024]{2,0,1:T(8,128)}) %reduce-scatter.5.cloned.1.call-update) | async-done | bytes 2097168 | tf_op jit(solution)/shard_map/reduce_scatter | solution.py:161
  412.0 24.8 %all-gather.14.cloned.1.call-done = bf16[1024,1024]{1,0:T(8,128)(2,1)} async-done(((bf16[128,1024]{1,0:T(8,128)(2,1)}), bf16[1024,1024]{1,0:T(8,128)(2,1)}) %all-gather.14.cloned.1.call-update) | async-done | bytes 2097168 | tf_op jit(solution)/shard_map/all_gather | solution.py:135
  436.9 82.8 %all-gather.12.cloned.1.call-done = bf16[2048,1,1024]{2,0,1:T(8,128)(2,1)} async-done(((bf16[512,1,1024]{2,0,1:T(8,128)(2,1)}), bf16[2048,1,1024]{2,0,1:T(8,128)(2,1)}) %all-gather.12.cloned.1.call-update) | async-done | bytes 4194320 | tf_op jit(solution)/shard_map/all_gather | solution.py:152
  519.6 25.3 %fusion.38 = (f32[2048,1024]{1,0:T(8,128)}, f32[2048,1024]{1,0:T(8,128)}) fusion(f32[1024]{0:T(1024)S(1)} %convert_element_type.117, bf16[1024,1024]{1,0:T(8,128)(2,1)} %all-gather.14.cloned.1.call-done, bf16[2048,1,1024]{2,0,1:T(8,128)(2,1)} %all-gather.12.cloned.1.call-done), kind=kOutput, calls=%fused_computation.53 | convolution fusion | flops 4427087872 | bytes 23072768 | tf_op jit(solution)/shard_map/nrd,df->nrf/dot_general | solution.py:150
  548.0 14.1 convolution_bitcast_fusion.1
  562.6 144.3 %reduce-scatter.7.cloned.1.call-done = f32[512,1,1024]{2,0,1:T(8,128)} async-done(((f32[2048,1,1024]{2,0,1:T(8,128)}), f32[512,1,1024]{2,0,1:T(8,128)}) %reduce-scatter.7.cloned.1.call-update) | async-done | bytes 2097168 | tf_op jit(solution)/shard_map/reduce_scatter | solution.py:170
  715.0 81.4 %all-gather.18.cloned.1.call-done = bf16[2048,1,1024]{2,0,1:T(8,128)(2,1)} async-done(((bf16[512,1,1024]{2,0,1:T(8,128)(2,1)}), bf16[2048,1,1024]{2,0,1:T(8,128)(2,1)}) %all-gather.18.cloned.1.call-update) | async-done | bytes 4194320 | tf_op jit(solution)/shard_map/all_gather | solution.py:181
  796.4 18.0 %convolution_bitcast_fusion = f32[2048,1,1024]{2,0,1:T(8,128)} fusion(bf16[1024,1024]{1,0:T(8,128)(2,1)} %all-gather.14.cloned.1.call-done, f32[2048,1024]{1,0:T(8,128)} %get-tuple-element.325, f32[2048,1024]{1,0:T(8,128)} %get-tuple-element.326, f32[1024]{0:T(1024)S(1)} %convert_element_type.117, bf16[1024,1024]{1,0:T(8,128)(2,1)} %all-gather.16.cloned.1.call-done, ...), kind=kOutput, calls=%fused_computation.71 | convolution fusion | flops 8621391872 | bytes 33558528 | tf_op jit(solution)/shard_map/nrf,df->nrd/dot_general | solution.py:191
  814.5 143.2 %reduce-scatter.9.cloned.1.call-done = f32[512,1,1024]{2,0,1:T(8,128)} async-done(((f32[2048,1,1024]{2,0,1:T(8,128)}), f32[512,1,1024]{2,0,1:T(8,128)}) %reduce-scatter.9.cloned.1.call-update) | async-done | bytes 2097168 | tf_op jit(solution)/shard_map/reduce_scatter | solution.py:190
  965.8 81.4 %all-gather.20.cloned.1.call-done = bf16[2048,1,1024]{2,0,1:T(8,128)(2,1)} async-done(((bf16[512,1,1024]{2,0,1:T(8,128)(2,1)}), bf16[2048,1,1024]{2,0,1:T(8,128)(2,1)}) %all-gather.20.cloned.1.call-update) | async-done | bytes 4194320 | tf_op jit(solution)/shard_map/all_gather | solution.py:201
  1061.5 239.9 %while.48 = (s32[]{:T(128)}, f32[2112,4,64]{0,2,1:T(8,128)}, f32[2112,4,64]{0,2,1:T(8,128)}, bf16[4,512,4,64]{1,3,2,0:T(8,128)(2,1)}, bf16[4,512,4,64]{1,3,2,0:T...) while((s32[]{:T(128)}, f32[2112,4,64]{0,2,1:T(8,128)}, ...), condition=%wide.region_19.20_spmd.clone, body=%wide.region_17.19_spmd.clone.sunk | while | flops 2813379072 | bytes 179895344 | solution.py:119
  1072.5 12.5 multiply_reduce_fusion.6
  1084.9 15.5 %multiply_convert_fusion.4 = bf16[4,512,2112]{1,2,0:T(8,128)(2,1)} fusion(f32[4,512,2112]{1,2,0:T(8,128)} %get-tuple-element.451, f32[4,512,2112]{1,2,0:T(8,128)} %fusion.132, f32[4,512]{1,0:T(4,128)S(1)} %get-tuple-element.452), kind=kLoop, calls=%fused_computation.20.clone.1 | loop fusion | flops 12976128 | bytes 43261952 | tf_op jit(solution)/shard_map/while/body/eval_jaxpr/while/body/eval_jaxpr/convert_element_type | solution.py:94
  1131.5 12.5 multiply_reduce_fusion.6
  1143.9 15.5 %multiply_convert_fusion.4 = bf16[4,512,2112]{1,2,0:T(8,128)(2,1)} fusion(f32[4,512,2112]{1,2,0:T(8,128)} %get-tuple-element.451, f32[4,512,2112]{1,2,0:T(8,128)} %fusion.132, f32[4,512]{1,0:T(4,128)S(1)} %get-tuple-element.452), kind=kLoop, calls=%fused_computation.20.clone.1 | loop fusion | flops 12976128 | bytes 43261952 | tf_op jit(solution)/shard_map/while/body/eval_jaxpr/while/body/eval_jaxpr/convert_element_type | solution.py:94
  1191.7 12.5 multiply_reduce_fusion.6
  1204.1 15.5 %multiply_convert_fusion.4 = bf16[4,512,2112]{1,2,0:T(8,128)(2,1)} fusion(f32[4,512,2112]{1,2,0:T(8,128)} %get-tuple-element.451, f32[4,512,2112]{1,2,0:T(8,128)} %fusion.132, f32[4,512]{1,0:T(4,128)S(1)} %get-tuple-element.452), kind=kLoop, calls=%fused_computation.20.clone.1 | loop fusion | flops 12976128 | bytes 43261952 | tf_op jit(solution)/shard_map/while/body/eval_jaxpr/while/body/eval_jaxpr/convert_element_type | solution.py:94
  1251.9 12.5 multiply_reduce_fusion.6
  1264.4 15.5 %multiply_convert_fusion.4 = bf16[4,512,2112]{1,2,0:T(8,128)(2,1)} fusion(f32[4,512,2112]{1,2,0:T(8,128)} %get-tuple-element.451, f32[4,512,2112]{1,2,0:T(8,128)} %fusion.132, f32[4,512]{1,0:T(4,128)S(1)} %get-tuple-element.452), kind=kLoop, calls=%fused_computation.20.clone.1 | loop fusion | flops 12976128 | bytes 43261952 | tf_op jit(solution)/shard_map/while/body/eval_jaxpr/while/body/eval_jaxpr/convert_element_type | solution.py:94
  1320.3 44.5 %all-reduce.4.cloned.1.call-done = (bf16[64,256]{1,0:T(8,128)(2,1)}, bf16[64,256]{1,0:T(8,128)(2,1)}) async-done(((bf16[64,256]{1,0:T(8,128)(2,1)}, bf16[64,256]{1,0:T(8,128)(2,1)}), (bf16[64,256]{1,0:T(8,128)(2,1)}, bf16[64,256]{1,0:T(8,128)(2,1)})) %all-reduce.4.cloned.1.call-update) | async-done | bytes 65552 | tf_op jit(solution)/shard_map/psum | solution.py:287
  1367.5 75.6 %reduce-scatter.11.cloned.1.call-done = bf16[512,1,1024]{2,0,1:T(8,128)(2,1)} async-done(((bf16[2048,1,1024]{2,0,1:T(8,128)(2,1)}), bf16[512,1,1024]{2,0,1:T(8,128)(2,1)}) %reduce-scatter.11.cloned.1.call-update) | async-done | bytes 1048592 | tf_op jit(solution)/shard_map/reduce_scatter | solution.py:210
  (202 shorter events, 352.9 us)
Async XLA Ops:
  7.2 33.1 %all-gather.10.cloned.1.call-start = ((), (), s32[]{:S(2)}) async-start(), calls=%async_computation.5 | async-start | bytes 1769472 | tf_op jit(solution)/shard_map/all_gather | solution.py:133
  9.0 113.6 %all-gather.8.cloned.1.call-start = ((), (), s32[]{:S(2)}) async-start(), calls=%async_computation.4 | async-start | bytes 5242880 | tf_op jit(solution)/shard_map/all_gather | solution.py:141
  9.7 397.0 %reduce-scatter.5.cloned.1.call-start = ((), (), s32[]{:S(2)}) async-start(), calls=%async_computation.6 | async-start | bytes 10485760 | tf_op jit(solution)/shard_map/reduce_scatter | solution.py:161
  263.4 143.3 %copy-start.10 = (bf16[512,1,1024]{2,0,1:T(8,128)(2,1)S(1)}, bf16[512,1,1024]{2,0,1:T(8,128)(2,1)}, u32[]{:S(2)}) copy-start(bf16[512,1,1024]{2,0,1:T(8,128)(2,1)} %param.18) | copy-start | bytes 3145732
  263.4 173.4 %all-gather.14.cloned.1.call-start = ((), (), s32[]{:S(2)}) async-start(), calls=%async_computation.8 | async-start | bytes 2359296 | tf_op jit(solution)/shard_map/all_gather | solution.py:135
  264.0 255.6 %all-gather.12.cloned.1.call-start = ((), (), s32[]{:S(2)}) async-start(), calls=%async_computation.7 | async-start | bytes 5242880 | tf_op jit(solution)/shard_map/all_gather | solution.py:152
  411.4 136.6 %all-gather.16.cloned.1.call-start = ((), (), s32[]{:S(2)}) async-start(), calls=%async_computation.9 | async-start | bytes 2359296 | tf_op jit(solution)/shard_map/all_gather | solution.py:136
  412.0 295.0 %reduce-scatter.7.cloned.1.call-start = ((), (), s32[]{:S(2)}) async-start(), calls=%async_computation.10 | async-start | bytes 10485760 | tf_op jit(solution)/shard_map/reduce_scatter | solution.py:170
  562.2 147.7 %copy-start.11 = (bf16[512,1,1024]{2,0,1:T(8,128)(2,1)S(1)}, bf16[512,1,1024]{2,0,1:T(8,128)(2,1)}, u32[]{:S(2)}) copy-start(bf16[512,1,1024]{2,0,1:T(8,128)(2,1)} %param.19) | copy-start | bytes 3145732
  562.2 234.3 %all-gather.18.cloned.1.call-start = ((), (), s32[]{:S(2)}) async-start(), calls=%async_computation.11 | async-start | bytes 5242880 | tf_op jit(solution)/shard_map/all_gather | solution.py:181
  714.9 242.7 %reduce-scatter.9.cloned.1.call-start = ((), (), s32[]{:S(2)}) async-start(), calls=%async_computation.12 | async-start | bytes 10485760 | tf_op jit(solution)/shard_map/reduce_scatter | solution.py:190
  814.4 232.8 %all-gather.20.cloned.1.call-start = ((), (), s32[]{:S(2)}) async-start(), calls=%async_computation.13 | async-start | bytes 5242880 | tf_op jit(solution)/shard_map/all_gather | solution.py:201
  963.2 84.0 %copy-start.13 = (bf16[256,1024]{1,0:T(8,128)(2,1)S(1)}, bf16[256,1024]{1,0:T(8,128)(2,1)}, u32[]{:S(2)}) copy-start(bf16[256,1024]{1,0:T(8,128)(2,1)} %all_gather.32) | copy-start | bytes 1572868
  963.3 88.5 %copy-start.14 = (f32[512]{0:T(512)}, f32[512]{0:T(512)S(1)}, u32[]{:S(2)}) copy-start(f32[512]{0:T(512)S(1)} %negate_multiply_fusion.1) | copy-start | bytes 6148
  965.7 399.0 %all-reduce.4.cloned.1.call-start = ((), (), s32[]{:S(2)}) async-start(), calls=%async_computation.15 | async-start | bytes 131072 | tf_op jit(solution)/shard_map/psum | solution.py:287
  1051.8 9.8 copy-start.5
  1100.5 7.6 copy-start
  1159.4 8.2 copy-start
  1219.7 8.2 copy-start
  1279.9 8.2 copy-start
  1303.6 6.3 copy-start.9
  1312.8 130.3 %reduce-scatter.11.cloned.1.call-start = ((), (), s32[]{:S(2)}) async-start(), calls=%async_computation.14 | async-start | bytes 5242880 | tf_op jit(solution)/shard_map/reduce_scatter | solution.py:210
  1320.2 122.8 %copy-start.7 = (f32[512,1,1024]{2,0,1:T(8,128)S(1)}, f32[512,1,1024]{2,0,1:T(8,128)}, u32[]{:S(2)}) copy-start(f32[512,1,1024]{2,0,1:T(8,128)} %copy-done.6) | copy-start | bytes 6291460
  1320.2 122.8 %copy-start.15 = (f32[512]{0:T(512)S(1)}, f32[512]{0:T(512)}, u32[]{:S(2)}) copy-start(f32[512]{0:T(512)} %copy-done.14) | copy-start | bytes 6148
  (11 other events, 24.2 us)
Sparse Core Ops, SparseCore 0:
  10.4 29.8 all-gather.9
  41.8 80.7 all-gather.7
  263.6 143.1 reduce-scatter.4
  408.5 28.3 all-gather.13
  438.9 80.7 all-gather.11
  521.4 26.5 all-gather.15
  562.3 144.6 reduce-scatter.6
  715.1 81.3 all-gather.17
  814.6 143.0 reduce-scatter.8
  965.9 81.3 all-gather.19
  1312.9 51.8 all-reduce.3
  1366.9 76.1 reduce-scatter.10
where the time goes:
time: 1460 us
  waiting for transfers between devices  920 us (63%)
  matrix products  327 us (22%)
  other arithmetic  141 us (10%)
  local copies, waits for them, and re-layouts  36.2 us (2%)
  between operations  14.8 us (1%)
  blocking collectives  14.6 us (1%)
    reduce_scatter x1, waiting for transfers between devices, reduce_down(): lax.psum_scatter(jnp.einsum('nrf,fd->nrd', active, down_full, preferred_e...  144 us
    reduce_scatter x1, waiting for transfers between devices, up_back(): lax.psum_scatter(jnp.einsum('nrf,df->nrd', grad_hidden, up_full, preferre...  143 us
    reduce_scatter x1, waiting for transfers between devices, mix_heads(): lax.psum_scatter(jnp.einsum('nrk,kd->nrd', mixed, out_full, preferred_ele...  143 us
    dot_general x8, matrix products, block_scores(): jnp.einsum('qhd,khd->hqk', query_block, keys_all, preferred_element_type=...  85.1 us
    all_gather x1, waiting for transfers between devices, expand(): lax.all_gather(normed_low, 'tp', axis=0, tiled=True)  82.8 us
    all_gather x1, waiting for transfers between devices, project_inputs(): piece = lax.all_gather(hidden, 'tp', axis=0, tiled=True)  82.3 us
    all_gather x1, waiting for transfers between devices, output_back(): lax.all_gather(grad_low, 'tp', axis=0, tiled=True)  81.4 us
    all_gather x1, waiting for transfers between devices, mixing_back(): lax.all_gather(grad_low, 'tp', axis=0, tiled=True)  81.4 us
  transfers between devices with their start and end apart: 12, of which 12 were waited for; matrix products, arithmetic and copies ran while one was open for 3% of the time, Pallas kernels for 0%

commit v1 on v0

--- a/solution.py
+++ b/solution.py
@@ -284,7 +284,7 @@
     key_local = jnp.sum(key_grads, axis=0).reshape(PREFIX, width)
     value_local = jnp.sum(value_grads, axis=0).reshape(PREFIX, width)
     key_total, value_total = (
-        lax.psum(key_local.astype(jnp.bfloat16), "rows").astype(jnp.float32),
+        jnp.sum(lax.all_gather(key_local.astype(jnp.bfloat16), "rows"), axis=0).astype(jnp.float32),
         lax.psum(value_local.astype(jnp.bfloat16), "rows").astype(jnp.float32),
     )
     return (result.astype(jnp.bfloat16), grad_input, key_total, value_total)

time: 1460 us -> 1410 us (0.966)
  waiting for transfers between devices: 920 us -> 839 us
  blocking collectives: 14.6 us -> 49.3 us
    psum x1 -> x0, waiting for transfers between devices: 44.5 us -> none  [body(): lax.psum(key_local.astype(jnp.bfloat16), 'rows').astype(jnp.float32)]
    reduce_scatter x1, waiting for transfers between devices: 75.6 us -> 39.1 us  [input_back(): lax.psum_scatter(jnp.einsum('nrje,jde->nrd', piece, qkv_full, preferred_e...]
    psum x0 -> x1, blocking collectives: none -> 25.2 us  [body(): lax.psum(value_local.astype(jnp.bfloat16), 'rows').astype(jnp.float32)]
  transfers between devices with their start and end apart: 12 -> 11, of which waited for: 12 -> 11; matrix products, arithmetic and copies ran while one was open for 3% -> 2% of each run, Pallas kernels for 0% -> 0%
where the time goes in v1:
time: 1410 us
  waiting for transfers between devices  839 us (60%)
  matrix products  327 us (23%)
  other arithmetic  139 us (10%)
  blocking collectives  49.3 us (3%)
  local copies, waits for them, and re-layouts  39 us (3%)
  between operations  14.4 us (1%)
    reduce_scatter x1, waiting for transfers between devices, reduce_down(): lax.psum_scatter(jnp.einsum('nrf,fd->nrd', active, down_full, preferred_e...  144 us
    reduce_scatter x1, waiting for transfers between devices, up_back(): lax.psum_scatter(jnp.einsum('nrf,df->nrd', grad_hidden, up_full, preferre...  143 us
    reduce_scatter x1, waiting for transfers between devices, mix_heads(): lax.psum_scatter(jnp.einsum('nrk,kd->nrd', mixed, out_full, preferred_ele...  143 us
    dot_general x8, matrix products, block_scores(): jnp.einsum('qhd,khd->hqk', query_block, keys_all, preferred_element_type=...  85 us
    all_gather x1, waiting for transfers between devices, expand(): lax.all_gather(normed_low, 'tp', axis=0, tiled=True)  82.8 us
    all_gather x1, waiting for transfers between devices, project_inputs(): piece = lax.all_gather(hidden, 'tp', axis=0, tiled=True)  82.3 us
    all_gather x1, waiting for transfers between devices, mixing_back(): lax.all_gather(grad_low, 'tp', axis=0, tiled=True)  81.4 us
    all_gather x1, waiting for transfers between devices, output_back(): lax.all_gather(grad_low, 'tp', axis=0, tiled=True)  81.4 us
  transfers between devices with their start and end apart: 11, of which 11 were waited for; matrix products, arithmetic and copies ran while one was open for 2% of the time, Pallas kernels for 0%

profile of v1, /device:TPU:0, one launch (start us, length us, event | category | flops | bytes accessed | tf_op | source)
XLA Modules:
  0.0 1409.3 jit_solution(10785871733444868893)
XLA Ops:
  13.4 14.6 %all_gather.36 = bf16[256,1024]{1,0:T(8,128)(2,1)} all-gather(bf16[256,128]{1,0:T(8,128)(2,1)} %param.23), channel_id=1, replica_groups=mesh['rows'=8,'tp'=4] {'rows'}, dimensions={1}, use_global_device_ids=true | all-gather | bytes 589824 | tf_op jit(solution)/shard_map/all_gather | solution.py:134
  40.3 82.3 %all-gather.8.cloned.1.call-done = bf16[2048,1,1024]{2,0,1:T(8,128)(2,1)} async-done(((bf16[512,1,1024]{2,0,1:T(8,128)(2,1)}), bf16[2048,1,1024]{2,0,1:T(8,128)(2,1)}) %all-gather.8.cloned.1.call-update) | async-done | bytes 4194320 | tf_op jit(solution)/shard_map/all_gather | solution.py:141
  135.6 120.7 %while.47 = (s32[]{:T(128)}, bf16[4,512,4,64]{1,3,2,0:T(8,128)(2,1)}, f32[4,4,512]{2,1,0:T(4,128)S(1)}, s32[2112]{0:T(1024)S(1)}, s32[4,512]{1,0:T(4,128)S(1)}, ...) while((s32[]{:T(128)}, ...), condition=%wide.region_5.6_spmd, body=%wide.region_2.5_spmd.sunk | while | flops 1162576384 | bytes 59005412 | solution.py:70
  263.9 142.5 %reduce-scatter.5.cloned.1.call-done = f32[512,1,1024]{2,0,1:T(8,128)} async-done(((f32[2048,1,1024]{2,0,1:T(8,128)}), f32[512,1,1024]{2,0,1:T(8,128)}) %reduce-scatter.5.cloned.1.call-update) | async-done | bytes 2097168 | tf_op jit(solution)/shard_map/reduce_scatter | solution.py:161
  411.8 24.9 %all-gather.14.cloned.1.call-done = bf16[1024,1024]{1,0:T(8,128)(2,1)} async-done(((bf16[128,1024]{1,0:T(8,128)(2,1)}), bf16[1024,1024]{1,0:T(8,128)(2,1)}) %all-gather.14.cloned.1.call-update) | async-done | bytes 2097168 | tf_op jit(solution)/shard_map/all_gather | solution.py:135
  436.6 82.8 %all-gather.12.cloned.1.call-done = bf16[2048,1,1024]{2,0,1:T(8,128)(2,1)} async-done(((bf16[512,1,1024]{2,0,1:T(8,128)(2,1)}), bf16[2048,1,1024]{2,0,1:T(8,128)(2,1)}) %all-gather.12.cloned.1.call-update) | async-done | bytes 4194320 | tf_op jit(solution)/shard_map/all_gather | solution.py:152
  519.4 25.3 %fusion.38 = (f32[2048,1024]{1,0:T(8,128)}, f32[2048,1024]{1,0:T(8,128)}) fusion(f32[1024]{0:T(1024)S(1)} %convert_element_type.126, bf16[1024,1024]{1,0:T(8,128)(2,1)} %all-gather.14.cloned.1.call-done, bf16[2048,1,1024]{2,0,1:T(8,128)(2,1)} %all-gather.12.cloned.1.call-done), kind=kOutput, calls=%fused_computation.53 | convolution fusion | flops 4427087872 | bytes 23072768 | tf_op jit(solution)/shard_map/nrd,df->nrf/dot_general | solution.py:150
  547.8 14.1 %convolution_bitcast_fusion.1 = f32[2048,1,1024]{2,0,1:T(8,128)} fusion(bf16[1024,1024]{1,0:T(8,128)(2,1)} %all-gather.16.cloned.1.call-done, f32[2048,1024]{1,0:T(8,128)} %get-tuple-element.346, f32[2048,1024]{1,0:T(8,128)} %get-tuple-element.347, f32[1024]{0:T(1024)S(1)} %convert_element_type.126), kind=kOutput, calls=%fused_computation.72 | convolution fusion | flops 4303355904 | bytes 27267072 | tf_op jit(solution)/shard_map/nrf,fd->nrd/dot_general | solution.py:171
  562.4 144.3 %reduce-scatter.7.cloned.1.call-done = f32[512,1,1024]{2,0,1:T(8,128)} async-done(((f32[2048,1,1024]{2,0,1:T(8,128)}), f32[512,1,1024]{2,0,1:T(8,128)}) %reduce-scatter.7.cloned.1.call-update) | async-done | bytes 2097168 | tf_op jit(solution)/shard_map/reduce_scatter | solution.py:170
  714.7 81.4 %all-gather.18.cloned.1.call-done = bf16[2048,1,1024]{2,0,1:T(8,128)(2,1)} async-done(((bf16[512,1,1024]{2,0,1:T(8,128)(2,1)}), bf16[2048,1,1024]{2,0,1:T(8,128)(2,1)}) %all-gather.18.cloned.1.call-update) | async-done | bytes 4194320 | tf_op jit(solution)/shard_map/all_gather | solution.py:181
  796.2 17.9 %convolution_bitcast_fusion = f32[2048,1,1024]{2,0,1:T(8,128)} fusion(bf16[1024,1024]{1,0:T(8,128)(2,1)} %all-gather.14.cloned.1.call-done, f32[2048,1024]{1,0:T(8,128)} %get-tuple-element.346, f32[2048,1024]{1,0:T(8,128)} %get-tuple-element.347, f32[1024]{0:T(1024)S(1)} %convert_element_type.126, bf16[1024,1024]{1,0:T(8,128)(2,1)} %all-gather.16.cloned.1.call-done, ...), kind=kOutput, calls=%fused_computation.71 | convolution fusion | flops 8621391872 | bytes 33558528 | tf_op jit(solution)/shard_map/nrf,df->nrd/dot_general | solution.py:191
  814.2 143.2 %reduce-scatter.9.cloned.1.call-done = f32[512,1,1024]{2,0,1:T(8,128)} async-done(((f32[2048,1,1024]{2,0,1:T(8,128)}), f32[512,1,1024]{2,0,1:T(8,128)}) %reduce-scatter.9.cloned.1.call-update) | async-done | bytes 2097168 | tf_op jit(solution)/shard_map/reduce_scatter | solution.py:190
  965.5 81.4 %all-gather.20.cloned.1.call-done = bf16[2048,1,1024]{2,0,1:T(8,128)(2,1)} async-done(((bf16[512,1,1024]{2,0,1:T(8,128)(2,1)}), bf16[2048,1,1024]{2,0,1:T(8,128)(2,1)}) %all-gather.20.cloned.1.call-update) | async-done | bytes 4194320 | tf_op jit(solution)/shard_map/all_gather | solution.py:201
  1061.3 240.0 %while.48 = (s32[]{:T(128)}, f32[2112,4,64]{0,2,1:T(8,128)}, f32[2112,4,64]{0,2,1:T(8,128)}, bf16[4,512,4,64]{1,3,2,0:T(8,128)(2,1)}, bf16[4,512,4,64]{1,3,2,0:T...) while((s32[]{:T(128)}, f32[2112,4,64]{0,2,1:T(8,128)}, ...), condition=%wide.region_19.20_spmd.clone, body=%wide.region_17.19_spmd.clone.sunk | while | flops 2813379072 | bytes 179895344 | solution.py:119
  1072.2 12.5 multiply_reduce_fusion.6
  1084.7 15.5 %multiply_convert_fusion.4 = bf16[4,512,2112]{1,2,0:T(8,128)(2,1)} fusion(f32[4,512,2112]{1,2,0:T(8,128)} %get-tuple-element.472, f32[4,512,2112]{1,2,0:T(8,128)} %fusion.132, f32[4,512]{1,0:T(4,128)S(1)} %get-tuple-element.473), kind=kLoop, calls=%fused_computation.20.clone.1 | loop fusion | flops 12976128 | bytes 43261952 | tf_op jit(solution)/shard_map/while/body/eval_jaxpr/while/body/eval_jaxpr/convert_element_type | solution.py:94
  1131.2 12.5 multiply_reduce_fusion.6
  1143.7 15.5 %multiply_convert_fusion.4 = bf16[4,512,2112]{1,2,0:T(8,128)(2,1)} fusion(f32[4,512,2112]{1,2,0:T(8,128)} %get-tuple-element.472, f32[4,512,2112]{1,2,0:T(8,128)} %fusion.132, f32[4,512]{1,0:T(4,128)S(1)} %get-tuple-element.473), kind=kLoop, calls=%fused_computation.20.clone.1 | loop fusion | flops 12976128 | bytes 43261952 | tf_op jit(solution)/shard_map/while/body/eval_jaxpr/while/body/eval_jaxpr/convert_element_type | solution.py:94
  1191.5 12.5 multiply_reduce_fusion.6
  1204.0 15.5 %multiply_convert_fusion.4 = bf16[4,512,2112]{1,2,0:T(8,128)(2,1)} fusion(f32[4,512,2112]{1,2,0:T(8,128)} %get-tuple-element.472, f32[4,512,2112]{1,2,0:T(8,128)} %fusion.132, f32[4,512]{1,0:T(4,128)S(1)} %get-tuple-element.473), kind=kLoop, calls=%fused_computation.20.clone.1 | loop fusion | flops 12976128 | bytes 43261952 | tf_op jit(solution)/shard_map/while/body/eval_jaxpr/while/body/eval_jaxpr/convert_element_type | solution.py:94
  1251.7 12.5 multiply_reduce_fusion.6
  1264.2 15.5 %multiply_convert_fusion.4 = bf16[4,512,2112]{1,2,0:T(8,128)(2,1)} fusion(f32[4,512,2112]{1,2,0:T(8,128)} %get-tuple-element.472, f32[4,512,2112]{1,2,0:T(8,128)} %fusion.132, f32[4,512]{1,0:T(4,128)S(1)} %get-tuple-element.473), kind=kLoop, calls=%fused_computation.20.clone.1 | loop fusion | flops 12976128 | bytes 43261952 | tf_op jit(solution)/shard_map/while/body/eval_jaxpr/while/body/eval_jaxpr/convert_element_type | solution.py:94
  1332.6 25.2 %psum.7 = bf16[64,256]{1,0:T(8,128)(2,1)S(1)} all-reduce(bf16[64,256]{1,0:T(8,128)(2,1)S(1)} %copy.76), channel_id=1, replica_groups=mesh['rows'=8,'tp'=4] {'rows'}, use_global_device_ids=true, to_apply=%region_22.23 | all-reduce | flops 16384 | bytes 65536 | tf_op jit(solution)/shard_map/psum | solution.py:288
  1358.4 39.1 %reduce-scatter.11.cloned.1.call-done = bf16[512,1,1024]{2,0,1:T(8,128)(2,1)} async-done(((bf16[2048,1,1024]{2,0,1:T(8,128)(2,1)}), bf16[512,1,1024]{2,0,1:T(8,128)(2,1)}) %reduce-scatter.11.cloned.1.call-update) | async-done | bytes 1048592 | tf_op jit(solution)/shard_map/reduce_scatter | solution.py:210
  (204 shorter events, 362.9 us)
Async XLA Ops:
  7.2 33.1 %all-gather.10.cloned.1.call-start = ((), (), s32[]{:S(2)}) async-start(), calls=%async_computation.5 | async-start | bytes 1769472 | tf_op jit(solution)/shard_map/all_gather | solution.py:133
  9.0 113.6 %all-gather.8.cloned.1.call-start = ((), (), s32[]{:S(2)}) async-start(), calls=%async_computation.4 | async-start | bytes 5242880 | tf_op jit(solution)/shard_map/all_gather | solution.py:141
  9.7 396.7 %reduce-scatter.5.cloned.1.call-start = ((), (), s32[]{:S(2)}) async-start(), calls=%async_computation.6 | async-start | bytes 10485760 | tf_op jit(solution)/shard_map/reduce_scatter | solution.py:161
  263.2 143.3 %copy-start.10 = (bf16[512,1,1024]{2,0,1:T(8,128)(2,1)S(1)}, bf16[512,1,1024]{2,0,1:T(8,128)(2,1)}, u32[]{:S(2)}) copy-start(bf16[512,1,1024]{2,0,1:T(8,128)(2,1)} %param.18) | copy-start | bytes 3145732
  263.2 173.4 %all-gather.14.cloned.1.call-start = ((), (), s32[]{:S(2)}) async-start(), calls=%async_computation.8 | async-start | bytes 2359296 | tf_op jit(solution)/shard_map/all_gather | solution.py:135
  263.8 255.6 %all-gather.12.cloned.1.call-start = ((), (), s32[]{:S(2)}) async-start(), calls=%async_computation.7 | async-start | bytes 5242880 | tf_op jit(solution)/shard_map/all_gather | solution.py:152
  411.1 136.6 %all-gather.16.cloned.1.call-start = ((), (), s32[]{:S(2)}) async-start(), calls=%async_computation.9 | async-start | bytes 2359296 | tf_op jit(solution)/shard_map/all_gather | solution.py:136
  411.7 295.0 %reduce-scatter.7.cloned.1.call-start = ((), (), s32[]{:S(2)}) async-start(), calls=%async_computation.10 | async-start | bytes 10485760 | tf_op jit(solution)/shard_map/reduce_scatter | solution.py:170
  561.9 147.7 %copy-start.11 = (bf16[512,1,1024]{2,0,1:T(8,128)(2,1)S(1)}, bf16[512,1,1024]{2,0,1:T(8,128)(2,1)}, u32[]{:S(2)}) copy-start(bf16[512,1,1024]{2,0,1:T(8,128)(2,1)} %param.19) | copy-start | bytes 3145732
  561.9 234.3 %all-gather.18.cloned.1.call-start = ((), (), s32[]{:S(2)}) async-start(), calls=%async_computation.11 | async-start | bytes 5242880 | tf_op jit(solution)/shard_map/all_gather | solution.py:181
  714.7 242.7 %reduce-scatter.9.cloned.1.call-start = ((), (), s32[]{:S(2)}) async-start(), calls=%async_computation.12 | async-start | bytes 10485760 | tf_op jit(solution)/shard_map/reduce_scatter | solution.py:190
  814.2 232.8 %all-gather.20.cloned.1.call-start = ((), (), s32[]{:S(2)}) async-start(), calls=%async_computation.13 | async-start | bytes 5242880 | tf_op jit(solution)/shard_map/all_gather | solution.py:201
  957.4 4.7 copy-start.8
  963.0 84.0 %copy-start.13 = (bf16[256,1024]{1,0:T(8,128)(2,1)S(1)}, bf16[256,1024]{1,0:T(8,128)(2,1)}, u32[]{:S(2)}) copy-start(bf16[256,1024]{1,0:T(8,128)(2,1)} %all_gather.36) | copy-start | bytes 1572868
  963.0 88.5 %copy-start.14 = (f32[512]{0:T(512)}, f32[512]{0:T(512)S(1)}, u32[]{:S(2)}) copy-start(f32[512]{0:T(512)S(1)} %negate_multiply_fusion.1) | copy-start | bytes 6148
  965.5 432.1 %reduce-scatter.11.cloned.1.call-start = ((), (), s32[]{:S(2)}) async-start(), calls=%async_computation.14 | async-start | bytes 5242880 | tf_op jit(solution)/shard_map/reduce_scatter | solution.py:210
  1051.5 9.8 copy-start.5
  1100.2 7.6 copy-start
  1159.2 8.2 copy-start
  1219.5 8.2 copy-start
  1279.7 8.2 copy-start
  1322.1 10.4 slice-start
  1322.1 75.5 %copy-start.7 = (f32[512,1,1024]{2,0,1:T(8,128)S(1)}, f32[512,1,1024]{2,0,1:T(8,128)}, u32[]{:S(2)}) copy-start(f32[512,1,1024]{2,0,1:T(8,128)} %copy-done.6) | copy-start | bytes 6291460
  1322.1 75.5 %copy-start.15 = (f32[512]{0:T(512)S(1)}, f32[512]{0:T(512)}, u32[]{:S(2)}) copy-start(f32[512]{0:T(512)} %copy-done.14) | copy-start | bytes 6148
  (11 other events, 20.5 us)
Sparse Core Ops, SparseCore 0:
  10.4 29.8 all-gather.9
  41.8 80.7 all-gather.7
  263.3 143.0 reduce-scatter.4
  408.2 28.3 all-gather.13
  438.6 80.7 all-gather.11
  521.1 26.5 all-gather.15
  562.0 144.6 reduce-scatter.6
  714.8 81.3 all-gather.17
  814.3 143.0 reduce-scatter.8
  965.6 81.3 all-gather.19
  1322.2 75.2 reduce-scatter.10
